TPU v7x, 512 devices: a whole 4x8x8 slice. The times are simulated.
512 devices in a mesh: sec: 64 (over x, y, core), mp: 8 (over z).
Axes of the slice: x: 4, y: 8, z: 8, core: 2. Of those that a mesh axis runs over, the one named last changes fastest.
Arguments:
- inputs: bfloat16 [8192, 2048], P('sec'), may hold values from -6 to 6
- expert_w: bfloat16 [8, 2048, 1024], P('mp', 'sec'), may hold values from -0.125 to 0.125
- gate_w: bfloat16 [2048, 6, 8], replicated, may hold values from -0.125 to 0.125
- tower_up: bfloat16 [64, 1024, 4096], P('sec', None, 'mp'), as said below
- tower_out: bfloat16 [64, 4096], P('sec', 'mp'), as said below
- sections: int32 [64], replicated, may hold values from 0 to 5, as said below
- tasks: int32 [8192, 6], P('sec'), may hold values from 0 to 1, as said below
- labels: int32 [8192, 6], P('sec'), may hold values 0 or 1
Outputs:
- input_grad: bfloat16 [8192, 2048], P('sec', 'mp')
Inputs may be any that keep to these rules, and one draw needn't show every extreme that they name: `sections`: each task owns one run of consecutive indices, the runs in task order, every task at least one index. `tasks`: in each aligned block of 128 examples, task t has at most 4 times as many examples as its section has indices of sec; every task reaches this bound in some block. `tower_up`: all indices of one section hold equal copies. `tower_out`: all indices of one section hold equal copies.
All inputs are finite; a program needn't handle non-finite values. No bound on the sum of `labels` on one device may be relied on, other than what follows from the above.
Results may differ from a plain program's by a relative error of at most 0.024.
Values may be sent and summed in bfloat16 or wider, within the bound.
No kernel may reach another device: no remote copies, remote signals or barrier semaphores. Data moves between devices by JAX's collectives and lax.ppermute only.
A program may use at most 64 MiB of HBM per device.

v0:
```python
import jax
import jax.numpy as jnp
from jax import lax
from jax.sharding import PartitionSpec as P

loss_scale = 64.0


def silu_slope(value, sig):
    return sig * (1.0 + value * (1.0 - sig))


def per_device(inputs, expert_w, gate_w, tower_up, tower_out, sections, tasks, labels):
    rows = inputs.shape[0]
    task_count = tasks.shape[1]
    n_sec = lax.axis_size("sec")
    pair_slots = 2 * rows // n_sec
    slots = n_sec * pair_slots
    local_w = expert_w[0]
    width = local_w.shape[1]
    picker = (jnp.arange(gate_w.shape[2], dtype=jnp.int32) == lax.axis_index("mp")).astype(
        jnp.float32
    )
    gate_logit = jnp.einsum("nd,dtk->ntk", inputs, gate_w, preferred_element_type=jnp.float32)
    raised = jnp.exp(gate_logit)
    gates = raised / jnp.sum(raised, axis=2, keepdims=True)
    mine = jnp.sum(gates * picker, axis=2)
    whole_w = lax.all_gather(local_w, "sec", axis=0, tiled=True)
    pre = jnp.dot(inputs, whole_w, preferred_element_type=jnp.float32)
    sig_pre = jax.nn.sigmoid(pre)
    expert_out = (pre * sig_pre).astype(jnp.bfloat16)
    task_ids = jnp.arange(task_count, dtype=jnp.int32)
    members = jnp.sum((sections[None, :] == task_ids[:, None]).astype(jnp.int32), axis=1)
    first = jnp.sum((sections[None, :] < task_ids[:, None]).astype(jnp.int32), axis=1)
    ranks = jnp.cumsum(tasks, axis=0) - tasks
    target = first[None, :] + ranks % members[None, :]
    place = target * pair_slots + ranks // members[None, :]
    place = jnp.where(tasks > 0, place, slots)
    pair_total = rows * task_count
    pair_ids = jnp.arange(pair_total, dtype=jnp.int32)
    source = (
        jnp.full((slots,), pair_total, jnp.int32).at[place.reshape(-1)].set(pair_ids, mode="drop")
    )
    filled = (source < pair_total).astype(jnp.float32)
    source = jnp.minimum(source, pair_total - 1)
    src_row = source // task_count
    src_task = source % task_count
    weight = mine[src_row, src_task] * filled
    contrib = weight[:, None] * expert_out[src_row].astype(jnp.float32)
    tag_out = (filled * (1.0 + labels[src_row, src_task].astype(jnp.float32))).astype(jnp.bfloat16)
    sent = lax.psum(contrib.astype(jnp.bfloat16), "mp")
    arrived, tag_in = (
        lax.all_to_all(
            sent.reshape(n_sec, pair_slots, -1), "sec", split_axis=0, concat_axis=0, tiled=True
        ),
        lax.all_to_all(
            tag_out.reshape(n_sec, pair_slots), "sec", split_axis=0, concat_axis=0, tiled=True
        ),
    )
    arrived = arrived.reshape(slots, -1)
    up_local = tower_up[0]
    out_local = tower_out[0].astype(jnp.float32)
    act = jnp.dot(arrived, up_local, preferred_element_type=jnp.float32)
    sig_act = jax.nn.sigmoid(act)
    partial_logit = jnp.sum(act * sig_act * out_local[None, :], axis=1)
    logit = lax.psum(partial_logit, "mp")
    tag_value = tag_in.reshape(slots).astype(jnp.float32)
    alive = (tag_value > 0.5).astype(jnp.float32)
    label_value = jnp.maximum(tag_value - 1.0, 0.0)
    slope = loss_scale * (jax.nn.sigmoid(logit) - label_value) * alive
    act_grad = (slope[:, None] * out_local[None, :] * silu_slope(act, sig_act)).astype(jnp.bfloat16)
    back = lax.dot_general(
        act_grad, up_local, (((1,), (1,)), ((), ())), preferred_element_type=jnp.float32
    )
    grads = lax.psum(back.astype(jnp.bfloat16), "mp")
    returned = lax.all_to_all(
        grads.reshape(n_sec, pair_slots, -1), "sec", split_axis=0, concat_axis=0, tiled=True
    ).reshape(slots, -1)
    padded = jnp.concatenate([returned, jnp.zeros((1, width), jnp.bfloat16)], axis=0)
    mixture_grad = padded[place]
    expert_grad = jnp.zeros((rows, width), jnp.float32)
    for task in range(task_count):
        expert_grad = expert_grad + mine[:, task : task + 1] * mixture_grad[:, task].astype(
            jnp.float32
        )
    gate_grad = jnp.einsum(
        "nte,ne->nt", mixture_grad, expert_out, preferred_element_type=jnp.float32
    )
    spread_sum = lax.psum(mine * gate_grad, "mp")
    gate_logit_grad = mine * (gate_grad - spread_sum)
    pre_grad = (expert_grad * silu_slope(pre, sig_pre)).astype(jnp.bfloat16)
    gate_cols = jnp.sum(gate_w.astype(jnp.float32) * picker, axis=2)
    gate_part = jnp.dot(gate_logit_grad, gate_cols.T, precision=lax.Precision.HIGHEST)
    input_part = lax.dot_general(
        pre_grad, whole_w, (((1,), (1,)), ((), ())), preferred_element_type=jnp.float32
    )
    return lax.psum_scatter(
        (input_part + gate_part).astype(jnp.bfloat16), "mp", scatter_dimension=1, tiled=True
    )


def solution(mesh):
    in_specs = (
        P("sec", None),
        P("mp", "sec", None),
        P(),
        P("sec", None, "mp"),
        P("sec", "mp"),
        P(),
        P("sec", None),
        P("sec", None),
    )
    out_specs = P("sec", "mp")
    return jax.shard_map(
        per_device, mesh=mesh, in_specs=in_specs, out_specs=out_specs, check_vma=False
    )
```

profile of v0, /device:TPU:2, one launch (start us, length us, event | category | flops | bytes accessed | tf_op | source)
XLA Modules:
  0.0 409.1 jit_solution(17913889090033370645)
XLA Ops:
  6.5 0.7 all-gather.3.cloned.1.call-update
  7.3 0.8 copy.35
  8.1 0.7 broadcast_compare_fusion
  9.1 0.8 convert_reduce_fusion.1
  9.9 1.3 compare_select_fusion
  11.4 3.4 scatter_custom_fusion
  14.8 1.4 fusion.54
  16.3 1.4 gather_fusion.1
  17.6 1.4 gather_fusion
  19.1 79.5 %all-gather.3.cloned.1.call-done = bf16[1,2048,1024]{2,1,0:T(8,128)(2,1)} async-done(((bf16[1,32,1024]{2,1,0:T(8,128)(2,1)}), bf16[1,2048,1024]{2,1,0:T(8,128)(2,1)}) %all-gather.3.cloned.1.call-update) | async-done | bytes 4194320 | tf_op jit(solution)/shard_map/all_gather | solution.py:28
  98.6 3.8 multiply_convert_fusion.2
  102.4 1.2 gather_fusion.2
  103.7 1.0 reshape.94
  104.9 16.0 %all_to_all.20 = bf16[64,1,4]{2,1,0:T(2,128)(2,1)S(1)} all-to-all(bf16[64,1,4]{2,1,0:T(2,128)(2,1)S(1)} %all_to_all.16), channel_id=1, replica_groups=mesh['sec'=64,'mp'=8] {'sec'}, dimensions={0} | all-to-all | bytes 1024 | tf_op jit(solution)/shard_map/all_to_all | solution.py:56
  120.8 62.6 %all-reduce.4.cloned.1.call-done = bf16[64,4,1024]{2,1,0:T(4,128)(2,1)} async-done(((bf16[64,4,1024]{2,1,0:T(4,128)(2,1)}), bf16[64,4,1024]{2,1,0:T(4,128)(2,1)}) %all-reduce.4.cloned.1.call-update) | async-done | bytes 524304 | tf_op jit(solution)/shard_map/psum | solution.py:51
  183.4 10.3 %all-to-all-start.1 = ((bf16[64,4,1024]{2,1,0:T(4,128)(2,1)}), bf16[64,4,1024]{2,1,0:T(4,128)(2,1)S(1)}, u32[]{:S(2)}, u32[]{:S(2)}) async-start(bf16[64,4,1024]{2,1,0:T(4,128)(2,1)} %all-reduce.4.cloned.1.call-done), calls=%async_computation.1 | async-start | bytes 1048576 | tf_op jit(solution)/shard_map/all_to_all | solution.py:53
  194.3 16.1 %all-to-all-done.1 = bf16[64,4,1024]{2,1,0:T(4,128)(2,1)S(1)} async-done(((bf16[64,4,1024]{2,1,0:T(4,128)(2,1)}), bf16[64,4,1024]{2,1,0:T(4,128)(2,1)S(1)}, u32[]{:S(2)}, u32[]{:S(2)}) %all-to-all-start.1) | async-done | bytes 524320 | tf_op jit(solution)/shard_map/all_to_all | solution.py:53
  210.5 0.6 multiply_reduce_fusion
  211.1 16.3 %psum.29 = f32[256]{0:T(256)S(1)} all-reduce(f32[256]{0:T(256)S(1)} %get-tuple-element.29), channel_id=1, replica_groups=mesh['sec'=64,'mp'=8] {'mp'}, use_global_device_ids=true, to_apply=%region_8.9 | all-reduce | flops 256 | bytes 2048 | tf_op jit(solution)/shard_map/psum | solution.py:66
  227.4 0.7 convolution_convert_fusion
  228.1 1.0 reshape.96
  229.1 75.2 %all-reduce.6.cloned.1.call-done = bf16[64,4,1024]{2,1,0:T(4,128)(2,1)} async-done(((bf16[64,4,1024]{2,1,0:T(4,128)(2,1)}), bf16[64,4,1024]{2,1,0:T(4,128)(2,1)}) %all-reduce.6.cloned.1.call-update) | async-done | bytes 524304 | tf_op jit(solution)/shard_map/psum | solution.py:75
  304.4 10.3 %all-to-all-start.2 = ((bf16[64,4,1024]{2,1,0:T(4,128)(2,1)}), bf16[64,4,1024]{2,1,0:T(4,128)(2,1)S(1)}, u32[]{:S(2)}, u32[]{:S(2)}) async-start(bf16[64,4,1024]{2,1,0:T(4,128)(2,1)} %all-reduce.6.cloned.1.call-done), calls=%async_computation.2 | async-start | bytes 1048576 | tf_op jit(solution)/shard_map/all_to_all | solution.py:76
  315.8 15.5 %all-to-all-done.2 = bf16[64,4,1024]{2,1,0:T(4,128)(2,1)S(1)} async-done(((bf16[64,4,1024]{2,1,0:T(4,128)(2,1)}), bf16[64,4,1024]{2,1,0:T(4,128)(2,1)S(1)}, u32[]{:S(2)}, u32[]{:S(2)}) %all-to-all-start.2) | async-done | bytes 524320 | tf_op jit(solution)/shard_map/all_to_all | solution.py:76
  331.5 3.6 gather_fusion.3
  335.0 2.5 reshape.126
  337.5 3.7 fusion.53
  341.3 1.3 fusion.24
  342.7 16.3 %psum.31 = f32[128,6]{0,1:T(8,128)S(1)} all-reduce(f32[128,6]{0,1:T(8,128)S(1)} %bitcast_multiply_fusion), channel_id=1, replica_groups=mesh['sec'=64,'mp'=8] {'mp'}, use_global_device_ids=true, to_apply=%region_10.11 | all-reduce | flops 768 | bytes 6144 | tf_op jit(solution)/shard_map/psum | solution.py:89
  358.9 1.0 fusion.45
  360.0 6.1 %fusion.8 = bf16[128,2048]{1,0:T(8,128)(2,1)} fusion(f32[128,2048]{1,0:T(8,128)S(1)} %fusion.45, bf16[1,2048,1024]{2,1,0:T(8,128)(2,1)} %all-gather.3.cloned.1.call-done, f32[128,1024]{1,0:T(8,128)} %get-tuple-element.28, bf16[128,1,1024]{2,1,0:T(2,128)(2,1)} %get-tuple-element.16, bf16[128,1,1024]{2,1,0:T(2,128)(2,1)} %get-tuple-element.12, ...), kind=kOutput, calls=%fused_computation.11 | convolution fusion | flops 540803072 | bytes 7867392 | tf_op jit(solution)/shard_map/dot_general | solution.py:94
  366.1 36.4 %reduce-scatter.2.cloned.1.call-done = bf16[128,256]{1,0:T(8,128)(2,1)} async-done(((bf16[128,2048]{1,0:T(8,128)(2,1)}), bf16[128,256]{1,0:T(8,128)(2,1)}) %reduce-scatter.2.cloned.1.call-update) | async-done | bytes 65552 | tf_op jit(solution)/shard_map/reduce_scatter | solution.py:97
  (45 shorter events, 2.8 us)
Async XLA Ops:
  6.5 204.0 %copy-start = (bf16[1,1024,512]{2,1,0:T(8,128)(2,1)S(1)}, bf16[1,1024,512]{2,1,0:T(8,128)(2,1)}, u32[]{:S(2)}) copy-start(bf16[1,1024,512]{2,1,0:T(8,128)(2,1)} %param.11) | copy-start | bytes 3145732
  6.5 92.1 %copy-start.4 = (bf16[128,2048]{1,0:T(8,128)(2,1)S(1)}, bf16[128,2048]{1,0:T(8,128)(2,1)}, u32[]{:S(2)}) copy-start(bf16[128,2048]{1,0:T(8,128)(2,1)} %param.8) | copy-start | bytes 1572868
  6.5 11.1 %copy-start.1 = (s32[128,6]{0,1:T(8,128)S(1)}, s32[128,6]{0,1:T(8,128)}, u32[]{:S(2)}) copy-start(s32[128,6]{0,1:T(8,128)} %param.15) | copy-start | bytes 9220
  6.5 92.0 %all-gather.3.cloned.1.call-start = ((), (), s32[]{:S(2)}) async-start(), calls=%async_computation.7 | async-start | bytes 4259840 | tf_op jit(solution)/shard_map/all_gather | solution.py:28
  7.3 176.2 %all-reduce.4.cloned.1.call-start = ((), (), s32[]{:S(2)}) async-start(), calls=%async_computation.4 | async-start | bytes 1048576 | tf_op jit(solution)/shard_map/psum | solution.py:51
  103.5 90.3 %copy-start.3 = (bf16[1,512]{1,0:T(2,128)(2,1)S(1)}, bf16[1,512]{1,0:T(2,128)(2,1)}, u32[]{:S(2)}) copy-start(bf16[1,512]{1,0:T(2,128)(2,1)} %param.12) | copy-start | bytes 3076
  183.4 26.9 %all-to-all-start.1 = ((bf16[64,4,1024]{2,1,0:T(4,128)(2,1)}), bf16[64,4,1024]{2,1,0:T(4,128)(2,1)S(1)}, u32[]{:S(2)}, u32[]{:S(2)}) async-start(bf16[64,4,1024]{2,1,0:T(4,128)(2,1)} %all-reduce.4.cloned.1.call-done), calls=%async_computation.1 | async-start | bytes 1048576 | tf_op jit(solution)/shard_map/all_to_all | solution.py:53
  193.7 110.6 %all-reduce.6.cloned.1.call-start = ((), (), s32[]{:S(2)}) async-start(), calls=%async_computation.5 | async-start | bytes 1048576 | tf_op jit(solution)/shard_map/psum | solution.py:75
  228.1 87.0 %copy-start.2 = (bf16[2048,6,8]{0,2,1:T(8,128)(2,1)S(1)}, bf16[2048,6,8]{0,2,1:T(8,128)(2,1)}, u32[]{:S(2)}) copy-start(bf16[2048,6,8]{0,2,1:T(8,128)(2,1)} %param.10) | copy-start | bytes 589828
  304.4 26.9 %all-to-all-start.2 = ((bf16[64,4,1024]{2,1,0:T(4,128)(2,1)}), bf16[64,4,1024]{2,1,0:T(4,128)(2,1)S(1)}, u32[]{:S(2)}, u32[]{:S(2)}) async-start(bf16[64,4,1024]{2,1,0:T(4,128)(2,1)} %all-reduce.6.cloned.1.call-done), calls=%async_computation.2 | async-start | bytes 1048576 | tf_op jit(solution)/shard_map/all_to_all | solution.py:76
  314.6 87.9 %reduce-scatter.2.cloned.1.call-start = ((), (), s32[]{:S(2)}) async-start(), calls=%async_computation.6 | async-start | bytes 589824 | tf_op jit(solution)/shard_map/reduce_scatter | solution.py:97
Sparse Core Ops, SparseCore 0:
  10.7 87.8 all-gather.2
  104.9 78.5 all-reduce.3
  229.2 75.0 all-reduce.5
  366.2 36.2 reduce-scatter.1
where the time goes:
time: 410 us; the launch traced here: 409 us
  waiting for transfers between devices  286 us (70%)
  blocking collectives  48.5 us (12%)
  local copies, waits for them, and re-layouts  21.5 us (5%)
  starting transfers between devices  20.9 us (5%)
  matrix products  14.9 us (4%)
  between operations  13.4 us (3%)
    all_gather x1, waiting for transfers between devices, per_device(): whole_w = lax.all_gather(local_w, 'sec', axis=0, tiled=True)  79.5 us
    psum x1, waiting for transfers between devices, per_device(): grads = lax.psum(back.astype(jnp.bfloat16), 'mp')  75.2 us
    psum x1, waiting for transfers between devices, per_device(): sent = lax.psum(contrib.astype(jnp.bfloat16), 'mp')  62.6 us
    reduce_scatter x1, waiting for transfers between devices, per_device(): lax.psum_scatter((input_part + gate_part).astype(jnp.bfloat16), 'mp', sca...  36.4 us
    psum x1, blocking collectives, per_device(): logit = lax.psum(partial_logit, 'mp')  16.3 us
    psum x1, blocking collectives, per_device(): spread_sum = lax.psum(mine * gate_grad, 'mp')  16.3 us
    all_to_all x1, waiting for transfers between devices, per_device(): lax.all_to_all(sent.reshape(n_sec, pair_slots, -1), 'sec', split_axis=0,...  16.1 us
    all_to_all x1, blocking collectives, per_device(): lax.all_to_all(tag_out.reshape(n_sec, pair_slots), 'sec', split_axis=0, c...  16 us
  transfers between devices with their start and end apart: 6, of which 6 were waited for; matrix products, arithmetic and copies ran while one was open for 3% of the time, Pallas kernels for 0%

commit v1 on v0

--- a/solution.py
+++ b/solution.py
@@ -25,7 +25,9 @@
     raised = jnp.exp(gate_logit)
     gates = raised / jnp.sum(raised, axis=2, keepdims=True)
     mine = jnp.sum(gates * picker, axis=2)
-    whole_w = lax.all_gather(local_w, "sec", axis=0, tiled=True)
+    whole_w = jnp.concatenate(
+        lax.all_to_all(jnp.stack([local_w] * lax.axis_size("sec")), "sec", 0, 0), axis=0
+    )
     pre = jnp.dot(inputs, whole_w, preferred_element_type=jnp.float32)
     sig_pre = jax.nn.sigmoid(pre)
     expert_out = (pre * sig_pre).astype(jnp.bfloat16)

time: 410 us -> 429 us (1.046)
  starting transfers between devices: 20.9 us -> 32 us
  waiting for transfers between devices: 286 us -> 295 us
    all_to_all x0 -> x1, waiting for transfers between devices: none -> 86 us  [per_device(): lax.all_to_all(jnp.stack([local_w] * lax.axis_size('sec')), 'sec', 0, 0)]
    all_gather x1 -> x0, waiting for transfers between devices: 79.5 us -> none  [per_device(): whole_w = lax.all_gather(local_w, 'sec', axis=0, tiled=True)]
    all_to_all x0 -> x1, starting transfers between devices: none -> 11.1 us  [per_device(): lax.all_to_all(jnp.stack([local_w] * lax.axis_size('sec')), 'sec', 0, 0)]
  transfers between devices with their start and end apart: 6 -> 6, of which waited for: 6 -> 6; matrix products, arithmetic and copies ran while one was open for 3% -> 2% of each run, Pallas kernels for 0% -> 0%
where the time goes in v1:
time: 429 us; the launch traced here: 428 us
  waiting for transfers between devices  295 us (69%)
  blocking collectives  47.8 us (11%)
  starting transfers between devices  32 us (7%)
  local copies, waits for them, and re-layouts  24.3 us (6%)
  matrix products  13.8 us (3%)
  between operations  13.4 us (3%)
    all_to_all x1, waiting for transfers between devices, per_device(): lax.all_to_all(jnp.stack([local_w] * lax.axis_size('sec')), 'sec', 0, 0)  86 us
    psum x1, waiting for transfers between devices, per_device(): grads = lax.psum(back.astype(jnp.bfloat16), 'mp')  75.2 us
    psum x1, waiting for transfers between devices, per_device(): sent = lax.psum(contrib.astype(jnp.bfloat16), 'mp')  65.4 us
    reduce_scatter x1, waiting for transfers between devices, per_device(): lax.psum_scatter((input_part + gate_part).astype(jnp.bfloat16), 'mp', sca...  36.4 us
    psum x1, blocking collectives, per_device(): spread_sum = lax.psum(mine * gate_grad, 'mp')  16.3 us
    psum x1, blocking collectives, per_device(): logit = lax.psum(partial_logit, 'mp')  16.2 us
    all_to_all x1, waiting for transfers between devices, per_device(): lax.all_to_all(sent.reshape(n_sec, pair_slots, -1), 'sec', split_axis=0,...  16.1 us
    all_to_all x1, waiting for transfers between devices, per_device(): lax.all_to_all(grads.reshape(n_sec, pair_slots, -1), 'sec', split_axis=0,...  15.5 us
  transfers between devices with their start and end apart: 6, of which 6 were waited for; matrix products, arithmetic and copies ran while one was open for 2% of the time, Pallas kernels for 0%

profile of v1, /device:TPU:2, one launch (start us, length us, event | category | flops | bytes accessed | tf_op | source)
XLA Modules:
  0.0 428.4 jit_solution(2151596215609290752)
XLA Ops:
  6.5 3.4 stack.3
  10.0 11.1 %all-to-all-start.1 = ((bf16[64,32,1024]{2,1,0:T(8,128)(2,1)}), bf16[64,32,1024]{2,1,0:T(8,128)(2,1)}, u32[]{:S(2)}, u32[]{:S(2)}) async-start(bf16[64,32,1024]{2,1,0:T(8,128)(2,1)} %stack.3), calls=%async_computation.1 | async-start | bytes 8388608 | tf_op jit(solution)/shard_map/all_to_all | solution.py:29
  21.8 1.3 compare_select_fusion
  23.3 3.4 scatter_custom_fusion
  26.7 0.3 fusion.45
  27.1 1.4 gather_fusion.1
  28.5 1.4 gather_fusion
  29.9 86.0 %all-to-all-done.1 = bf16[64,32,1024]{2,1,0:T(8,128)(2,1)} async-done(((bf16[64,32,1024]{2,1,0:T(8,128)(2,1)}), bf16[64,32,1024]{2,1,0:T(8,128)(2,1)}, u32[]{:S(2)}, u32[]{:S(2)}) %all-to-all-start.1) | async-done | bytes 4194336 | tf_op jit(solution)/shard_map/all_to_all | solution.py:29
  115.9 3.8 multiply_convert_fusion.2
  119.7 1.2 gather_fusion.2
  121.0 1.0 reshape.99
  122.2 15.3 %all_to_all.25 = bf16[64,1,4]{2,1,0:T(2,128)(2,1)S(1)} all-to-all(bf16[64,1,4]{2,1,0:T(2,128)(2,1)S(1)} %all_to_all.20), channel_id=1, replica_groups=mesh['sec'=64,'mp'=8] {'sec'}, dimensions={0} | all-to-all | bytes 1024 | tf_op jit(solution)/shard_map/all_to_all | solution.py:58
  137.4 65.4 %all-reduce.4.cloned.1.call-done = bf16[64,4,1024]{2,1,0:T(4,128)(2,1)} async-done(((bf16[64,4,1024]{2,1,0:T(4,128)(2,1)}), bf16[64,4,1024]{2,1,0:T(4,128)(2,1)}) %all-reduce.4.cloned.1.call-update) | async-done | bytes 524304 | tf_op jit(solution)/shard_map/psum | solution.py:53
  202.9 10.3 %all-to-all-start.2 = ((bf16[64,4,1024]{2,1,0:T(4,128)(2,1)}), bf16[64,4,1024]{2,1,0:T(4,128)(2,1)S(1)}, u32[]{:S(2)}, u32[]{:S(2)}) async-start(bf16[64,4,1024]{2,1,0:T(4,128)(2,1)} %all-reduce.4.cloned.1.call-done), calls=%async_computation.2 | async-start | bytes 1048576 | tf_op jit(solution)/shard_map/all_to_all | solution.py:55
  213.7 16.1 %all-to-all-done.2 = bf16[64,4,1024]{2,1,0:T(4,128)(2,1)S(1)} async-done(((bf16[64,4,1024]{2,1,0:T(4,128)(2,1)}), bf16[64,4,1024]{2,1,0:T(4,128)(2,1)S(1)}, u32[]{:S(2)}, u32[]{:S(2)}) %all-to-all-start.2) | async-done | bytes 524320 | tf_op jit(solution)/shard_map/all_to_all | solution.py:55
  229.9 0.6 multiply_reduce_fusion
  230.6 16.2 %psum.29 = f32[256]{0:T(256)S(1)} all-reduce(f32[256]{0:T(256)S(1)} %get-tuple-element.29), channel_id=1, replica_groups=mesh['sec'=64,'mp'=8] {'mp'}, use_global_device_ids=true, to_apply=%region_8.9 | all-reduce | flops 256 | bytes 2048 | tf_op jit(solution)/shard_map/psum | solution.py:68
  246.8 0.6 convolution_convert_fusion
  247.4 1.0 reshape.101
  248.5 75.2 %all-reduce.6.cloned.1.call-done = bf16[64,4,1024]{2,1,0:T(4,128)(2,1)} async-done(((bf16[64,4,1024]{2,1,0:T(4,128)(2,1)}), bf16[64,4,1024]{2,1,0:T(4,128)(2,1)}) %all-reduce.6.cloned.1.call-update) | async-done | bytes 524304 | tf_op jit(solution)/shard_map/psum | solution.py:77
  323.7 10.3 %all-to-all-start.3 = ((bf16[64,4,1024]{2,1,0:T(4,128)(2,1)}), bf16[64,4,1024]{2,1,0:T(4,128)(2,1)S(1)}, u32[]{:S(2)}, u32[]{:S(2)}) async-start(bf16[64,4,1024]{2,1,0:T(4,128)(2,1)} %all-reduce.6.cloned.1.call-done), calls=%async_computation.3 | async-start | bytes 1048576 | tf_op jit(solution)/shard_map/all_to_all | solution.py:78
  333.9 0.2 reduce-scatter.2.cloned.1.call-start
  334.5 0.6 slice_bitcast_fusion.5
  335.1 15.5 %all-to-all-done.3 = bf16[64,4,1024]{2,1,0:T(4,128)(2,1)S(1)} async-done(((bf16[64,4,1024]{2,1,0:T(4,128)(2,1)}), bf16[64,4,1024]{2,1,0:T(4,128)(2,1)S(1)}, u32[]{:S(2)}, u32[]{:S(2)}) %all-to-all-start.3) | async-done | bytes 524320 | tf_op jit(solution)/shard_map/all_to_all | solution.py:78
  350.8 3.6 gather_fusion.3
  354.4 2.5 reshape.131
  356.8 3.7 fusion.44
  360.6 1.3 fusion.15
  362.0 16.3 %psum.31 = f32[128,6]{0,1:T(8,128)S(1)} all-reduce(f32[128,6]{0,1:T(8,128)S(1)} %bitcast_multiply_fusion), channel_id=1, replica_groups=mesh['sec'=64,'mp'=8] {'mp'}, use_global_device_ids=true, to_apply=%region_10.11 | all-reduce | flops 768 | bytes 6144 | tf_op jit(solution)/shard_map/psum | solution.py:91
  378.2 5.3 %fusion.17 = f32[128,2048]{1,0:T(8,128)S(1)} fusion(bf16[2048,1024]{1,0:T(8,128)(2,1)} %bitcast.4, f32[128,1024]{1,0:T(8,128)} %get-tuple-element.28, bf16[128,1,1024]{2,1,0:T(2,128)(2,1)} %get-tuple-element.16, bf16[128,1,1024]{2,1,0:T(2,128)(2,1)} %get-tuple-element.12, bf16[128,1,1024]{2,1,0:T(2,128)(2,1)} %get-tuple-element.13, ...), kind=kOutput, calls=%fused_computation.38 | convolution fusion | flops 540278784 | bytes 7343104 | tf_op jit(solution)/shard_map/dot_general | solution.py:96
  383.5 1.9 fusion.1
  385.4 36.4 %reduce-scatter.2.cloned.1.call-done = bf16[128,256]{1,0:T(8,128)(2,1)} async-done(((bf16[128,2048]{1,0:T(8,128)(2,1)}), bf16[128,256]{1,0:T(8,128)(2,1)}) %reduce-scatter.2.cloned.1.call-update) | async-done | bytes 65552 | tf_op jit(solution)/shard_map/reduce_scatter | solution.py:99
  (49 shorter events, 2.4 us)
Async XLA Ops:
  6.5 223.4 %copy-start = (bf16[1,1024,512]{2,1,0:T(8,128)(2,1)S(1)}, bf16[1,1024,512]{2,1,0:T(8,128)(2,1)}, u32[]{:S(2)}) copy-start(bf16[1,1024,512]{2,1,0:T(8,128)(2,1)} %param.11) | copy-start | bytes 3145732
  10.0 11.2 %copy-start.3 = (s32[128,6]{0,1:T(8,128)S(1)}, s32[128,6]{0,1:T(8,128)}, u32[]{:S(2)}) copy-start(s32[128,6]{0,1:T(8,128)} %param.14) | copy-start | bytes 9220
  10.0 11.7 %copy-start.6 = (s32[64]{0:T(128)S(1)}, s32[64]{0:T(128)}, u32[]{:S(2)}) copy-start(s32[64]{0:T(128)} %param.13) | copy-start | bytes 772
  10.0 16.7 %copy-start.2 = (bf16[2048,6,8]{0,2,1:T(8,128)(2,1)S(1)}, bf16[2048,6,8]{0,2,1:T(8,128)(2,1)}, u32[]{:S(2)}) copy-start(bf16[2048,6,8]{0,2,1:T(8,128)(2,1)} %param.10) | copy-start | bytes 589828
  10.0 16.7 %copy-start.5 = (bf16[128,2048]{1,0:T(8,128)(2,1)S(1)}, bf16[128,2048]{1,0:T(8,128)(2,1)}, u32[]{:S(2)}) copy-start(bf16[128,2048]{1,0:T(8,128)(2,1)} %param.8) | copy-start | bytes 1572868
  10.0 105.9 %all-to-all-start.1 = ((bf16[64,32,1024]{2,1,0:T(8,128)(2,1)}), bf16[64,32,1024]{2,1,0:T(8,128)(2,1)}, u32[]{:S(2)}, u32[]{:S(2)}) async-start(bf16[64,32,1024]{2,1,0:T(8,128)(2,1)} %stack.3), calls=%async_computation.1 | async-start | bytes 8388608 | tf_op jit(solution)/shard_map/all_to_all | solution.py:29
  21.1 7.3 %copy-start.1 = (s32[128,6]{0,1:T(8,128)S(1)}, s32[128,6]{0,1:T(8,128)}, u32[]{:S(2)}) copy-start(s32[128,6]{0,1:T(8,128)} %param.15) | copy-start | bytes 9220
  21.1 181.7 %all-reduce.4.cloned.1.call-start = ((), (), s32[]{:S(2)}) async-start(), calls=%async_computation.5 | async-start | bytes 1048576 | tf_op jit(solution)/shard_map/psum | solution.py:53
  120.8 92.4 %copy-start.4 = (bf16[1,512]{1,0:T(2,128)(2,1)S(1)}, bf16[1,512]{1,0:T(2,128)(2,1)}, u32[]{:S(2)}) copy-start(bf16[1,512]{1,0:T(2,128)(2,1)} %param.12) | copy-start | bytes 3076
  202.9 26.9 %all-to-all-start.2 = ((bf16[64,4,1024]{2,1,0:T(4,128)(2,1)}), bf16[64,4,1024]{2,1,0:T(4,128)(2,1)S(1)}, u32[]{:S(2)}, u32[]{:S(2)}) async-start(bf16[64,4,1024]{2,1,0:T(4,128)(2,1)} %all-reduce.4.cloned.1.call-done), calls=%async_computation.2 | async-start | bytes 1048576 | tf_op jit(solution)/shard_map/all_to_all | solution.py:55
  213.1 110.5 %all-reduce.6.cloned.1.call-start = ((), (), s32[]{:S(2)}) async-start(), calls=%async_computation.6 | async-start | bytes 1048576 | tf_op jit(solution)/shard_map/psum | solution.py:77
  323.7 26.9 %all-to-all-start.3 = ((bf16[64,4,1024]{2,1,0:T(4,128)(2,1)}), bf16[64,4,1024]{2,1,0:T(4,128)(2,1)S(1)}, u32[]{:S(2)}, u32[]{:S(2)}) async-start(bf16[64,4,1024]{2,1,0:T(4,128)(2,1)} %all-reduce.6.cloned.1.call-done), calls=%async_computation.3 | async-start | bytes 1048576 | tf_op jit(solution)/shard_map/all_to_all | solution.py:78
  333.9 87.9 %reduce-scatter.2.cloned.1.call-start = ((), (), s32[]{:S(2)}) async-start(), calls=%async_computation.7 | async-start | bytes 589824 | tf_op jit(solution)/shard_map/reduce_scatter | solution.py:99
Sparse Core Ops, SparseCore 0:
  122.2 80.6 all-reduce.3
  248.6 75.0 all-reduce.5
  385.5 36.2 reduce-scatter.1
